TPU v7x, 256 devices: a whole 4x4x8 slice. The times are simulated.
256 devices in a mesh: rows: 128 (over x, y_hi, z, core), cols: 2 (over y_lo).
Axes of the slice: x: 4, y: 4 (y_hi: 2, y_lo: 2; y = y_hi * 2 + y_lo), z: 8, core: 2. Of those that a mesh axis runs over, the one named last changes fastest.
Arguments:
- ancestor: bfloat16 [24576, 24576], P('rows', 'cols'), may hold values from -6 to 6
- panel_below: bfloat16 [2048, 512], P('rows'), may hold values from -0.0625 to 0.0625
- panel_beside: bfloat16 [2048, 512], P('rows'), may hold values from -0.0625 to 0.0625
- inverse_lower: bfloat16 [512, 512], replicated, may hold values from -3 to 3
- inverse_upper: bfloat16 [512, 512], replicated, may hold values from -3 to 3
- list_below: int32 [16], replicated, may hold values from 0 to 191, as said below
- list_beside: int32 [16], replicated, may hold values from 0 to 191, as said below
- second_below: bfloat16 [2048, 512], P('rows'), may hold values from -0.0625 to 0.0625
- second_beside: bfloat16 [2048, 512], P('rows'), may hold values from -0.0625 to 0.0625
- linked_below: bfloat16 [512, 512], replicated, may hold values from -0.0625 to 0.0625
- linked_beside: bfloat16 [512, 512], replicated, may hold values from -0.0625 to 0.0625
- second_lower: bfloat16 [512, 512], replicated, may hold values from -3 to 3
- second_upper: bfloat16 [512, 512], replicated, may hold values from -3 to 3
- blocks_below: int32 [16], replicated, may hold values from 0 to 191, as said below
- blocks_beside: int32 [16], replicated, may hold values from 0 to 191, as said below
Outputs:
- new_lower: bfloat16 [24576, 512], P('rows', 'cols')
- new_upper: bfloat16 [24576, 512], P(('cols', 'rows'))
- new_diagonal: bfloat16 [512, 512], P(None, 'cols')
- next_lower: bfloat16 [24576, 512], P('rows', 'cols')
- next_upper: bfloat16 [24576, 512], P(('cols', 'rows'))
- next_link: bfloat16 [512, 512], replicated
- next_diagonal: bfloat16 [512, 512], P(None, 'cols')
Inputs may be any that keep to these rules, and one draw needn't show every extreme that they name: `list_below`: 16 distinct block numbers in ascending order; block 0 and block 191 are always listed. `list_beside`: 16 distinct block numbers in ascending order; block 0 and block 191 are always listed. `blocks_below`: 16 distinct block numbers in ascending order; block 0 and block 191 are always listed. `blocks_beside`: 16 distinct block numbers in ascending order; block 0 and block 191 are always listed.
All inputs are finite; a program needn't handle non-finite values.
Results may differ from a plain program's by a relative error of at most 0.0077.
Values may be sent and summed in bfloat16 or wider, within the bound.
A program may use at most 128 MiB of HBM per device.

v0:
```python
import jax
import jax.numpy as jnp
from jax import lax
from jax.sharding import PartitionSpec as P

BLK = 128


def normalise(panel, inverse):
    return jnp.dot(panel, inverse, preferred_element_type=jnp.float32).astype(jnp.bfloat16)


def normalise_by_rows(panel, inverse):
    return lax.dot_general(
        panel, inverse, (((1,), (1,)), ((), ())), preferred_element_type=jnp.float32
    ).astype(jnp.bfloat16)


def inner_rows(left, right):
    return lax.dot_general(
        left, right, (((0,), (0,)), ((), ())), preferred_element_type=jnp.float32
    )


def own_half(panel, first_column, half_width):
    return lax.dynamic_slice_in_dim(panel, first_column, half_width, 1)


def listed_columns(tile, blocks, first_block):
    block_count = tile.shape[1] // BLK
    local_ids = blocks - first_block
    inside = jnp.logical_and(local_ids >= 0, local_ids < block_count)
    picked = jnp.take(
        tile.reshape(tile.shape[0], block_count, BLK),
        jnp.clip(local_ids, 0, block_count - 1),
        axis=1,
    )
    return (picked.reshape(tile.shape[0], blocks.shape[0] * BLK), jnp.repeat(inside, BLK))


def masked_product(picked, inside, panel):
    kept = jnp.where(inside[:, None], panel, jnp.zeros_like(panel))
    return jnp.dot(picked, kept, preferred_element_type=jnp.float32)


def listed_rows(strips, blocks):
    shaped = strips.reshape(strips.shape[0] // BLK, BLK, strips.shape[1])
    return jnp.take(shaped, blocks, axis=0).reshape(blocks.shape[0] * BLK, strips.shape[1])


def rows_onto(panel, blocks, first_row, row_count):
    global_rows = first_row + jnp.arange(row_count, dtype=jnp.int32)
    block_of = global_rows // BLK
    offset = global_rows % BLK
    matches = block_of[:, None] == blocks[None, :]
    position = jnp.sum(
        jnp.where(matches, jnp.arange(blocks.shape[0], dtype=jnp.int32)[None, :], 0), axis=1
    )
    present = jnp.any(matches, axis=1)
    picked = jnp.take(panel, position * BLK + offset, axis=0)
    return jnp.where(present[:, None], picked, jnp.zeros_like(picked))


def lower_block(partial_value):
    return (-lax.psum_scatter(partial_value, "cols", scatter_dimension=1, tiled=True)).astype(
        jnp.bfloat16
    )


def diag_block(base_value, picked_rows, lower_local):
    summed = lax.psum(inner_rows(picked_rows, lower_local), "rows")
    return (base_value - summed).astype(jnp.bfloat16)


def body(
    ancestor,
    panel_below,
    panel_beside,
    inverse_lower,
    inverse_upper,
    list_below,
    list_beside,
    second_below,
    second_beside,
    linked_below,
    linked_beside,
    second_lower,
    second_upper,
    blocks_below,
    blocks_beside,
):
    row_devices = lax.axis_size("rows")
    row_at = lax.axis_index("rows")
    col_at = lax.axis_index("cols")
    col_devices = lax.axis_size("cols")
    tile_rows = ancestor.shape[0]
    tile_cols = ancestor.shape[1]
    width = inverse_lower.shape[0]
    half_width = width // col_devices
    first_column = col_at * half_width
    unit_below = normalise(panel_below, inverse_lower)
    unit_beside = normalise_by_rows(panel_beside, inverse_upper)
    below_next = normalise(second_below, second_lower)
    beside_next = normalise_by_rows(second_beside, second_upper)
    unit_below, unit_beside, below_next, beside_next = (
        lax.all_gather(unit_below, "rows", axis=0, tiled=True),
        lax.all_gather(unit_beside, "rows", axis=0, tiled=True),
        lax.all_gather(below_next, "rows", axis=0, tiled=True),
        lax.all_gather(beside_next, "rows", axis=0, tiled=True),
    )
    strips = lax.all_to_all(ancestor, "rows", split_axis=1, concat_axis=0, tiled=True)
    strip_width = tile_cols // row_devices
    strip_start = (col_at * row_devices + row_at) * strip_width
    first_block = col_at * (tile_cols // BLK)
    row_start = row_at * tile_rows
    picked, inside = listed_columns(ancestor, list_below, first_block)
    new_lower = lower_block(masked_product(picked, inside, unit_below))
    new_upper = (-inner_rows(listed_rows(strips, list_beside), unit_beside)).astype(jnp.bfloat16)
    base_first = jnp.dot(
        inverse_upper,
        own_half(inverse_lower, first_column, half_width),
        preferred_element_type=jnp.float32,
    )
    new_diagonal = diag_block(
        base_first, rows_onto(unit_beside, list_beside, row_start, tile_rows), new_lower
    )
    link_below = normalise(linked_below, second_lower)
    link_beside = normalise_by_rows(linked_beside, second_upper)
    link_rows = lax.dynamic_slice_in_dim(link_below, first_column, half_width, 0)
    picked_next, inside_next = listed_columns(ancestor, blocks_below, first_block)
    partial_value = masked_product(picked_next, inside_next, below_next) + jnp.dot(
        new_lower, link_rows, preferred_element_type=jnp.float32
    )
    next_lower = lower_block(partial_value)
    first_row = (row_at == 0).astype(jnp.float32)
    link_term = inner_rows(
        new_upper, rows_onto(below_next, blocks_below, strip_start, strip_width)
    ) + first_row * jnp.dot(new_diagonal, link_rows, preferred_element_type=jnp.float32)
    next_link = (-lax.psum(link_term, ("rows", "cols"))).astype(jnp.bfloat16)
    next_upper = (
        -(
            inner_rows(listed_rows(strips, blocks_beside), beside_next)
            + jnp.dot(new_upper, link_beside, preferred_element_type=jnp.float32)
        )
    ).astype(jnp.bfloat16)
    base_second = jnp.dot(
        second_upper,
        own_half(second_lower, first_column, half_width),
        preferred_element_type=jnp.float32,
    ) - inner_rows(link_beside, own_half(next_link, first_column, half_width))
    next_diagonal = diag_block(
        base_second, rows_onto(beside_next, blocks_beside, row_start, tile_rows), next_lower
    )
    return (new_lower, new_upper, new_diagonal, next_lower, next_upper, next_link, next_diagonal)


def solution(mesh):
    return jax.shard_map(
        body,
        mesh=mesh,
        in_specs=(
            P("rows", "cols"),
            P("rows", None),
            P("rows", None),
            P(),
            P(),
            P(),
            P(),
            P("rows", None),
            P("rows", None),
            P(),
            P(),
            P(),
            P(),
            P(),
            P(),
        ),
        out_specs=(
            P("rows", "cols"),
            P(("cols", "rows"), None),
            P(None, "cols"),
            P("rows", "cols"),
            P(("cols", "rows"), None),
            P(),
            P(None, "cols"),
        ),
        check_vma=False,
    )
```

profile of v0, /device:TPU:2, one launch (start us, length us, event | category | flops | bytes accessed | tf_op | source)
XLA Modules:
  0.0 2101.3 jit_solution(3499471611282957993)
XLA Ops:
  7.2 1.9 convolution_convert_fusion.4
  9.2 1.5 convolution_convert_fusion.2
  10.8 0.7 compare_and_fusion.2
  11.5 5.8 copy_bitcast_fusion
  17.3 3.0 gather_fusion.1
  20.4 110.8 %all-gather.5.cloned.1.call-done = bf16[2048,512]{1,0:T(8,128)(2,1)} async-done(((bf16[16,512]{1,0:T(8,128)(2,1)}), bf16[2048,512]{1,0:T(8,128)(2,1)}) %all-gather.5.cloned.1.call-update) | async-done | bytes 2097168 | tf_op jit(solution)/shard_map/all_gather | solution.py:106
  131.3 3.1 fusion.2
  134.4 0.9 convolution_convert_fusion.1
  135.3 10.1 all_to_all.12
  145.3 9.5 copy.76
  154.8 9.5 all-to-all-start
  164.4 0.9 convolution_convert_fusion.3
  165.4 3.0 gather_fusion.4
  168.8 0.4 fusion.66
  169.3 86.8 %all-gather.9.cloned.1.call-done = bf16[2048,512]{1,0:T(8,128)(2,1)} async-done(((bf16[16,512]{1,0:T(8,128)(2,1)}), bf16[2048,512]{1,0:T(8,128)(2,1)}) %all-gather.9.cloned.1.call-update) | async-done | bytes 2097168 | tf_op jit(solution)/shard_map/all_gather | solution.py:108
  256.1 2.2 fusion
  258.3 20.8 reduce-scatter.3.cloned.1.call-done
  279.1 0.9 negate_convert_fusion.2
  280.1 1.0 convolution_add_fusion.1
  281.6 120.8 %all-gather.11.cloned.1.call-done = bf16[2048,512]{1,0:T(8,128)(2,1)} async-done(((bf16[16,512]{1,0:T(8,128)(2,1)}), bf16[2048,512]{1,0:T(8,128)(2,1)}) %all-gather.11.cloned.1.call-update) | async-done | bytes 2097168 | tf_op jit(solution)/shard_map/all_gather | solution.py:109
  402.4 2.9 gather_fusion.6
  405.3 114.1 %all-gather.7.cloned.1.call-done = bf16[2048,512]{1,0:T(8,128)(2,1)} async-done(((bf16[16,512]{1,0:T(8,128)(2,1)}), bf16[2048,512]{1,0:T(8,128)(2,1)}) %all-gather.7.cloned.1.call-update) | async-done | bytes 2097168 | tf_op jit(solution)/shard_map/all_gather | solution.py:107
  519.4 2.9 gather_fusion.3
  522.3 1.1 fusion.30
  523.5 13.4 reduce-scatter.5.cloned.1.call-done
  536.9 0.9 negate_convert_fusion.1
  537.9 0.6 copy-done.14
  538.5 1.1 fusion.29
  539.7 0.5 compare_and_fusion.6
  540.3 0.5 compare_and_fusion.4
  540.8 1.5 convolution_convert_fusion
  542.3 3.3 gather_fusion
  545.6 1206.7 %all-reduce.6.cloned.1.call-done = (f32[512,256]{0,1:T(8,128)}, f32[512,256]{0,1:T(8,128)}) async-done(((f32[512,256]{0,1:T(8,128)}, f32[512,256]{0,1:T(8,128)}), (f32[512,256]{0,1:T(8,128)}, f32[512,256]{0,1:T(8,128)})) %all-reduce.6.cloned.1.call-update) | async-done | bytes 1048592 | tf_op jit(solution)/shard_map/psum | solution.py:71
  1752.3 1.4 fusion.10
  1753.7 0.8 copy.87
  1754.6 1.3 convolution_multiply_fusion
  1755.9 8.2 copy.78
  1764.1 3.0 gather_fusion.2
  1767.1 1.3 fusion.12
  1768.4 0.6 copy-done.11
  1769.0 1.3 convolution_add_fusion
  1770.4 3.0 gather_fusion.5
  1773.4 0.5 fusion.20
  1774.3 0.9 fusion.13
  1775.1 315.4 %all-reduce.4.cloned.1.call-done = f32[512,512]{1,0:T(8,128)} async-done(((f32[512,512]{1,0:T(8,128)}), f32[512,512]{1,0:T(8,128)}) %all-reduce.4.cloned.1.call-update) | async-done | bytes 1048592 | tf_op jit(solution)/shard_map/psum | solution.py:139
  2090.5 1.3 negate_convert_fusion
  2092.2 1.4 fusion.9
  2093.6 0.8 copy.88
  (78 shorter events, 2.1 us)
Async XLA Ops:
  7.2 2.0 copy-start
  7.2 124.1 %all-gather.5.cloned.1.call-start = ((), (), s32[]{:S(2)}) async-start(), calls=%async_computation.3 | async-start | bytes 2113536 | tf_op jit(solution)/shard_map/all_gather | solution.py:106
  9.2 246.9 %all-gather.9.cloned.1.call-start = ((), (), s32[]{:S(2)}) async-start(), calls=%async_computation.6 | async-start | bytes 2113536 | tf_op jit(solution)/shard_map/all_gather | solution.py:108
  10.7 268.4 %reduce-scatter.3.cloned.1.call-start = ((), (), s32[]{:S(2)}) async-start(), calls=%async_computation.4 | async-start | bytes 589824 | tf_op jit(solution)/shard_map/reduce_scatter | solution.py:65
  131.2 3.1 copy-start.2
  131.2 3.1 copy-start.15
  134.3 268.1 %all-gather.11.cloned.1.call-start = ((), (), s32[]{:S(2)}) async-start(), calls=%async_computation.8 | async-start | bytes 2113536 | tf_op jit(solution)/shard_map/all_gather | solution.py:109
  154.8 9.6 copy-start.5
  154.8 9.6 copy-start.16
  154.8 1601.1 %all-to-all-start = ((bf16[192,128,96]{2,0,1:T(8,128)(2,1)}), bf16[192,128,96]{2,0,1:T(8,128)(2,1)}, u32[]{:S(2)}, u32[]{:S(2)}) async-start(bf16[192,128,96]{2,0,1:T(8,128)(2,1)} %copy.76), calls=%async_computation.1 | async-start | bytes 12582912 | tf_op jit(solution)/shard_map/all_to_all | solution.py:111
  164.3 4.2 copy-start.17
  164.3 4.2 copy-start.18
  164.3 4.3 copy-start.19
  164.3 4.5 copy-start.10
  164.3 355.1 %all-gather.7.cloned.1.call-start = ((), (), s32[]{:S(2)}) async-start(), calls=%async_computation.5 | async-start | bytes 2113536 | tf_op jit(solution)/shard_map/all_gather | solution.py:107
  165.3 371.6 %reduce-scatter.5.cloned.1.call-start = ((), (), s32[]{:S(2)}) async-start(), calls=%async_computation.7 | async-start | bytes 589824 | tf_op jit(solution)/shard_map/reduce_scatter | solution.py:65
  280.1 242.2 %copy-start.9 = (bf16[192,256]{1,0:T(8,128)(2,1)}, bf16[192,256]{1,0:T(8,128)(2,1)S(1)}, u32[]{:S(2)}) copy-start(bf16[192,256]{1,0:T(8,128)(2,1)S(1)} %negate_convert_fusion.2) | copy-start | bytes 294916
  281.1 1471.2 %all-reduce.6.cloned.1.call-start = ((), (), s32[]{:S(2)}) async-start(), calls=%async_computation.10 | async-start | bytes 2097152 | tf_op jit(solution)/shard_map/psum | solution.py:71
  537.8 0.6 copy-start.14
  538.5 1213.9 %copy-start.8 = (bf16[512,512]{1,0:T(8,128)(2,1)S(1)}, bf16[512,512]{1,0:T(8,128)(2,1)}, u32[]{:S(2)}) copy-start(bf16[512,512]{1,0:T(8,128)(2,1)} %param.24) | copy-start | bytes 1572868
  539.7 1550.8 %all-reduce.4.cloned.1.call-start = ((), (), s32[]{:S(2)}) async-start(), calls=%async_computation.9 | async-start | bytes 2097152 | tf_op jit(solution)/shard_map/psum | solution.py:139
  1755.9 11.2 copy-start.7
  1767.1 1.9 copy-start.4
  1767.1 1.9 copy-start.13
  1767.1 1.9 copy-start.20
  1768.4 0.6 copy-start.11
  1769.0 4.3 copy-start.1
  1773.4 0.9 copy-start.12
  1774.3 318.0 %copy-start.3 = (bf16[512,512]{1,0:T(8,128)(2,1)S(1)}, bf16[512,512]{1,0:T(8,128)(2,1)}, u32[]{:S(2)}) copy-start(bf16[512,512]{1,0:T(8,128)(2,1)} %param.33) | copy-start | bytes 1572868
  2091.8 2.6 copy-start.6
Sparse Core Ops, SparseCore 0:
  12.3 118.9 all-gather.4
  135.5 120.4 all-gather.8
  259.2 19.9 reduce-scatter.2
  283.3 119.0 all-gather.10
  406.5 112.8 all-gather.6
  521.7 15.1 reduce-scatter.4
  540.1 1212.1 all-reduce.5
  1770.5 319.9 all-reduce.3
where the time goes:
time: 2100 us
  waiting for transfers between devices  1990 us (95%)
  local copies, waits for them, and re-layouts  58.2 us (3%)
  matrix products  24.1 us (1%)
    psum x1, waiting for transfers between devices, diag_block(): summed = lax.psum(inner_rows(picked_rows, lower_local), 'rows')  1210 us
    psum x1, waiting for transfers between devices, body(): next_link = (-lax.psum(link_term, ('rows', 'cols'))).astype(jnp.bfloat16)  315 us
    all_gather x1, waiting for transfers between devices, body(): lax.all_gather(beside_next, 'rows', axis=0, tiled=True)  121 us
    all_gather x1, waiting for transfers between devices, body(): lax.all_gather(unit_beside, 'rows', axis=0, tiled=True)  114 us
    all_gather x1, waiting for transfers between devices, body(): lax.all_gather(unit_below, 'rows', axis=0, tiled=True)  111 us
    all_gather x1, waiting for transfers between devices, body(): lax.all_gather(below_next, 'rows', axis=0, tiled=True)  86.8 us
  transfers between devices with their start and end apart: 9, of which 8 were waited for; matrix products, arithmetic and copies ran while one was open for 3% of the time, Pallas kernels for 0%

commit v1 on v0

--- a/solution.py
+++ b/solution.py
@@ -68,7 +68,8 @@
 
 
 def diag_block(base_value, picked_rows, lower_local):
-    summed = lax.psum(inner_rows(picked_rows, lower_local), "rows")
+    here_x = inner_rows(picked_rows, lower_local)
+    summed = jax.lax.all_gather(here_x, "rows").sum(axis=0)
     return (base_value - summed).astype(jnp.bfloat16)
 
 

time: 2100 us -> 1500 us (0.71)
  waiting for transfers between devices: 1990 us -> 1340 us
  other arithmetic: 5.43 us -> 46.3 us
    psum x1 -> x0, waiting for transfers between devices: 1210 us -> none  [diag_block(): summed = lax.psum(inner_rows(picked_rows, lower_local), 'rows')]
    all_gather x0 -> x2, waiting for transfers between devices: none -> 592 us  [diag_block(): summed = jax.lax.all_gather(here_x, 'rows').sum(axis=0)]
    psum x1, waiting for transfers between devices: 315 us -> 255 us  [body(): next_link = (-lax.psum(link_term, ('rows', 'cols'))).astype(jnp.bfloat16)]
    all_to_all x1, waiting for transfers between devices: 0.01 us -> 59.9 us  [body(): lax.all_to_all(ancestor, 'rows', split_axis=1, concat_axis=0, tiled=True)]
    reduce_sum x0 -> x2, other arithmetic: none -> 41.9 us  [diag_block(): summed = jax.lax.all_gather(here_x, 'rows').sum(axis=0)]
    all_gather x1, waiting for transfers between devices: 121 us -> 93.3 us  [body(): lax.all_gather(beside_next, 'rows', axis=0, tiled=True)]
  transfers between devices with their start and end apart: 9 -> 10, of which waited for: 8 -> 10; matrix products, arithmetic and copies ran while one was open for 3% -> 6% of each run, Pallas kernels for 0% -> 0%
where the time goes in v1:
time: 1500 us
  waiting for transfers between devices  1340 us (89%)
  local copies, waits for them, and re-layouts  57.7 us (4%)
  other arithmetic  46.3 us (3%)
  matrix products  23.4 us (2%)
    all_gather x2, waiting for transfers between devices, diag_block(): summed = jax.lax.all_gather(here_x, 'rows').sum(axis=0)  592 us
    psum x1, waiting for transfers between devices, body(): next_link = (-lax.psum(link_term, ('rows', 'cols'))).astype(jnp.bfloat16)  255 us
    all_gather x1, waiting for transfers between devices, body(): lax.all_gather(unit_beside, 'rows', axis=0, tiled=True)  113 us
    all_gather x1, waiting for transfers between devices, body(): lax.all_gather(unit_below, 'rows', axis=0, tiled=True)  110 us
    all_gather x1, waiting for transfers between devices, body(): lax.all_gather(beside_next, 'rows', axis=0, tiled=True)  93.3 us
    all_gather x1, waiting for transfers between devices, body(): lax.all_gather(below_next, 'rows', axis=0, tiled=True)  86.8 us
    all_to_all x1, waiting for transfers between devices, body(): lax.all_to_all(ancestor, 'rows', split_axis=1, concat_axis=0, tiled=True)  59.9 us
    reduce_sum x2, other arithmetic, diag_block(): summed = jax.lax.all_gather(here_x, 'rows').sum(axis=0)  41.9 us
  transfers between devices with their start and end apart: 10, of which 10 were waited for; matrix products, arithmetic and copies ran while one was open for 6% of the time, Pallas kernels for 0%

profile of v1, /device:TPU:2, one launch (start us, length us, event | category | flops | bytes accessed | tf_op | source)
XLA Modules:
  0.0 1496.3 jit_solution(17057768629103593012)
XLA Ops:
  7.2 1.9 convolution_convert_fusion.4
  9.2 1.9 convolution_convert_fusion.3
  11.2 0.7 compare_and_fusion.5
  11.9 5.9 copy_bitcast_fusion
  17.7 3.0 gather_fusion.1
  20.8 110.4 %all-gather.9.cloned.1.call-done = bf16[2048,512]{1,0:T(8,128)(2,1)} async-done(((bf16[16,512]{1,0:T(8,128)(2,1)}), bf16[2048,512]{1,0:T(8,128)(2,1)}) %all-gather.9.cloned.1.call-update) | async-done | bytes 2097168 | tf_op jit(solution)/shard_map/all_gather | solution.py:107
  131.3 3.0 fusion.2
  134.4 0.8 convolution_convert_fusion.2
  135.5 112.9 %all-gather.11.cloned.1.call-done = bf16[2048,512]{1,0:T(8,128)(2,1)} async-done(((bf16[16,512]{1,0:T(8,128)(2,1)}), bf16[2048,512]{1,0:T(8,128)(2,1)}) %all-gather.11.cloned.1.call-update) | async-done | bytes 2097168 | tf_op jit(solution)/shard_map/all_gather | solution.py:108
  248.4 2.9 gather_fusion.3
  251.3 15.3 %reduce-scatter.3.cloned.1.call-done = f32[192,256]{1,0:T(8,128)} async-done(((f32[192,512]{1,0:T(8,128)}), f32[192,256]{1,0:T(8,128)}) %reduce-scatter.3.cloned.1.call-update) | async-done | bytes 196624 | tf_op jit(solution)/shard_map/reduce_scatter | solution.py:65
  266.6 0.9 negate_convert_fusion.2
  267.6 1.2 fusion.30
  268.8 10.1 all_to_all.12
  278.8 9.4 copy.68
  288.3 14.1 all-to-all-start
  302.5 0.9 convolution_convert_fusion.1
  303.7 3.0 gather_fusion.4
  307.1 0.4 fusion.66
  307.5 86.8 %all-gather.13.cloned.1.call-done = bf16[2048,512]{1,0:T(8,128)(2,1)} async-done(((bf16[16,512]{1,0:T(8,128)(2,1)}), bf16[2048,512]{1,0:T(8,128)(2,1)}) %all-gather.13.cloned.1.call-update) | async-done | bytes 2097168 | tf_op jit(solution)/shard_map/all_gather | solution.py:109
  394.3 3.3 gather_fusion
  397.6 2.2 fusion
  399.9 1.0 convolution_add_fusion.1
  400.9 59.9 %all-to-all-done = bf16[192,128,96]{2,0,1:T(8,128)(2,1)} async-done(((bf16[192,128,96]{2,0,1:T(8,128)(2,1)}), bf16[192,128,96]{2,0,1:T(8,128)(2,1)}, u32[]{:S(2)}, u32[]{:S(2)}) %all-to-all-start) | async-done | bytes 4718624 | tf_op jit(solution)/shard_map/all_to_all | solution.py:112
  460.8 8.0 copy.70
  468.8 3.0 gather_fusion.2
  471.8 2.1 fusion.12
  474.0 266.3 %all-gather.17.cloned.1.call-done = f32[65536,256]{1,0:T(8,128)} async-done(((f32[512,256]{1,0:T(8,128)}), f32[65536,256]{1,0:T(8,128)}) %all-gather.17.cloned.1.call-update) | async-done | bytes 67108880 | tf_op jit(solution)/shard_map/all_gather | solution.py:72
  740.2 21.0 %reduce_sum.46 = f32[512,256]{1,0:T(8,128)S(1)} reduce(f32[128,512,256]{2,1,0:T(8,128)} %bitcast.5, f32[]{:T(128)} %constant.124.clone.1), dimensions={0}, to_apply=%region_3.7 | reduce | flops 16646144 | bytes 67633152 | tf_op jit(solution)/shard_map/reduce_sum | solution.py:72
  761.4 0.4 fusion.10
  762.3 1.4 convolution_add_fusion
  763.8 93.3 %all-gather.15.cloned.1.call-done = bf16[2048,512]{1,0:T(8,128)(2,1)} async-done(((bf16[16,512]{1,0:T(8,128)(2,1)}), bf16[2048,512]{1,0:T(8,128)(2,1)}) %all-gather.15.cloned.1.call-update) | async-done | bytes 2097168 | tf_op jit(solution)/shard_map/all_gather | solution.py:110
  857.1 2.9 gather_fusion.6
  860.0 14.7 reduce-scatter.5.cloned.1.call-done
  874.7 0.9 negate_convert_fusion.1
  875.7 1.2 fusion.29
  876.9 1.7 convolution_convert_fusion
  878.6 3.7 gather_fusion.5
  882.3 1.5 fusion.20
  883.8 0.9 fusion.13
  884.6 0.8 copy.79
  885.5 254.5 %all-reduce.2.cloned.1.call-done = f32[512,512]{1,0:T(8,128)} async-done(((f32[512,512]{1,0:T(8,128)}), f32[512,512]{1,0:T(8,128)}) %all-reduce.2.cloned.1.call-update) | async-done | bytes 1048592 | tf_op jit(solution)/shard_map/psum | solution.py:140
  1140.0 1.3 negate_convert_fusion
  1141.4 0.3 fusion.25
  1141.7 325.7 %all-gather.19.cloned.1.call-done = f32[65536,256]{1,0:T(8,128)} async-done(((f32[512,256]{1,0:T(8,128)}), f32[65536,256]{1,0:T(8,128)}) %all-gather.19.cloned.1.call-update) | async-done | bytes 67108880 | tf_op jit(solution)/shard_map/all_gather | solution.py:72
  1467.4 20.9 %reduce_sum.49 = f32[512,256]{1,0:T(8,128)S(1)} reduce(f32[128,512,256]{2,1,0:T(8,128)} %bitcast.12, f32[]{:T(128)} %constant.124.clone.1), dimensions={0}, to_apply=%region_10.14 | reduce | flops 16646144 | bytes 67633152 | tf_op jit(solution)/shard_map/reduce_sum | solution.py:72
  1488.6 0.4 fusion.9
  1488.9 0.8 copy.80
  (78 shorter events, 2.4 us)
Async XLA Ops:
  7.2 127.2 %copy-start = (bf16[512,512]{1,0:T(8,128)(2,1)S(1)}, bf16[512,512]{1,0:T(8,128)(2,1)}, u32[]{:S(2)}) copy-start(bf16[512,512]{1,0:T(8,128)(2,1)} %param.32) | copy-start | bytes 1572868
  7.2 124.1 %all-gather.9.cloned.1.call-start = ((), (), s32[]{:S(2)}) async-start(), calls=%async_computation.3 | async-start | bytes 2113536 | tf_op jit(solution)/shard_map/all_gather | solution.py:107
  9.2 239.2 %all-gather.11.cloned.1.call-start = ((), (), s32[]{:S(2)}) async-start(), calls=%async_computation.5 | async-start | bytes 2113536 | tf_op jit(solution)/shard_map/all_gather | solution.py:108
  11.1 255.5 %reduce-scatter.3.cloned.1.call-start = ((), (), s32[]{:S(2)}) async-start(), calls=%async_computation.4 | async-start | bytes 589824 | tf_op jit(solution)/shard_map/reduce_scatter | solution.py:65
  131.2 3.1 copy-start.12
  131.2 4.0 copy-start.14
  131.3 4.0 copy-start.15
  134.3 260.0 %all-gather.13.cloned.1.call-start = ((), (), s32[]{:S(2)}) async-start(), calls=%async_computation.6 | async-start | bytes 2113536 | tf_op jit(solution)/shard_map/all_gather | solution.py:109
  135.2 605.0 %all-gather.17.cloned.1.call-start = ((), (), s32[]{:S(2)}) async-start(), calls=%async_computation.10 | async-start | bytes 67633152 | tf_op jit(solution)/shard_map/all_gather | solution.py:72
  267.6 132.3 %copy-start.10 = (bf16[192,256]{1,0:T(8,128)(2,1)}, bf16[192,256]{1,0:T(8,128)(2,1)S(1)}, u32[]{:S(2)}) copy-start(bf16[192,256]{1,0:T(8,128)(2,1)S(1)} %negate_convert_fusion.2) | copy-start | bytes 294916
  288.3 14.2 copy-start.2
  288.3 14.2 copy-start.13
  288.3 15.3 %copy-start.16 = (s32[16]{0:T(128)S(1)}, s32[16]{0:T(128)}, u32[]{:S(2)}) copy-start(s32[16]{0:T(128)} %param.34) | copy-start | bytes 196
  288.3 172.5 %all-to-all-start = ((bf16[192,128,96]{2,0,1:T(8,128)(2,1)}), bf16[192,128,96]{2,0,1:T(8,128)(2,1)}, u32[]{:S(2)}, u32[]{:S(2)}) async-start(bf16[192,128,96]{2,0,1:T(8,128)(2,1)} %copy.68), calls=%async_computation.1 | async-start | bytes 12582912 | tf_op jit(solution)/shard_map/all_to_all | solution.py:112
  302.4 4.7 copy-start.7
  302.4 554.6 %all-gather.15.cloned.1.call-start = ((), (), s32[]{:S(2)}) async-start(), calls=%async_computation.8 | async-start | bytes 2113536 | tf_op jit(solution)/shard_map/all_gather | solution.py:110
  303.4 571.3 %reduce-scatter.5.cloned.1.call-start = ((), (), s32[]{:S(2)}) async-start(), calls=%async_computation.7 | async-start | bytes 589824 | tf_op jit(solution)/shard_map/reduce_scatter | solution.py:65
  400.9 739.1 %all-reduce.2.cloned.1.call-start = ((), (), s32[]{:S(2)}) async-start(), calls=%async_computation.9 | async-start | bytes 2097152 | tf_op jit(solution)/shard_map/psum | solution.py:140
  473.9 409.8 %copy-start.8 = (bf16[96,512]{1,0:T(8,128)(2,1)}, bf16[96,512]{1,0:T(8,128)(2,1)S(1)}, u32[]{:S(2)}) copy-start(bf16[96,512]{1,0:T(8,128)(2,1)S(1)} %fusion.12) | copy-start | bytes 294916
  740.2 21.2 %copy-start.4 = (bf16[512,512]{1,0:T(8,128)(2,1)S(1)}, bf16[512,512]{1,0:T(8,128)(2,1)}, u32[]{:S(2)}) copy-start(bf16[512,512]{1,0:T(8,128)(2,1)} %param.25) | copy-start | bytes 1572868
  740.2 21.2 %copy-start.6 = (bf16[512,512]{1,0:T(8,128)(2,1)S(1)}, bf16[512,512]{1,0:T(8,128)(2,1)}, u32[]{:S(2)}) copy-start(bf16[512,512]{1,0:T(8,128)(2,1)} %param.24) | copy-start | bytes 1572868
  761.4 0.9 copy-start.9
  763.7 703.7 %all-gather.19.cloned.1.call-start = ((), (), s32[]{:S(2)}) async-start(), calls=%async_computation.11 | async-start | bytes 67633152 | tf_op jit(solution)/shard_map/all_gather | solution.py:72
  860.0 22.3 %copy-start.1 = (bf16[2048,512]{1,0:T(8,128)(2,1)S(1)}, bf16[2048,512]{1,0:T(8,128)(2,1)}, u32[]{:S(2)}) copy-start(bf16[2048,512]{1,0:T(8,128)(2,1)} %all-gather.15.cloned.1.call-done) | copy-start | bytes 6291460
  875.7 1.2 copy-start.11
  1141.4 326.1 %copy-start.5 = (bf16[512,512]{1,0:T(8,128)(2,1)}, bf16[512,512]{1,0:T(8,128)(2,1)S(1)}, u32[]{:S(2)}) copy-start(bf16[512,512]{1,0:T(8,128)(2,1)S(1)} %negate_convert_fusion) | copy-start | bytes 1572868
  1467.4 21.1 %copy-start.3 = (bf16[512,512]{1,0:T(8,128)(2,1)S(1)}, bf16[512,512]{1,0:T(8,128)(2,1)}, u32[]{:S(2)}) copy-start(bf16[512,512]{1,0:T(8,128)(2,1)} %param.33) | copy-start | bytes 1572868
Sparse Core Ops, SparseCore 0:
  12.3 118.9 all-gather.8
  135.5 112.8 all-gather.10
  251.5 15.1 reduce-scatter.2
  270.8 123.4 all-gather.12
  398.4 341.7 all-gather.16
  744.4 112.6 all-gather.14
  859.6 15.1 reduce-scatter.4
  880.2 259.8 all-reduce.1
  1143.7 323.6 all-gather.18
